TPU v7x, 128 devices: a whole 4x4x4 slice. The times are simulated.
128 devices in a mesh: group: 8 (over y, core), dev: 16 (over z, x).
Axes of the slice: x: 4, y: 4, z: 4, core: 2. Of those that a mesh axis runs over, the one named last changes fastest.
Arguments:
- primary_q: bfloat16 [256, 3584, 1024], P(('group', 'dev')), may hold values from -0.09375 to 0.09375
- primary_scales: bfloat16 [256, 28, 8], P(('group', 'dev')), may hold values from 0.5 to 2
- new_place: int32 [128], P(('group', 'dev')), may hold values from 0 to 255, as said below
- tokens: bfloat16 [2048, 3584], P(('group', 'dev')), may hold values from -6 to 6
- experts: int32 [2048, 8], P(('group', 'dev')), may hold values from 0 to 255, all different within a row
- replica: int32 [2048, 8], P(('group', 'dev')), may hold values from 0 to 1
- route_num: int32 [2048, 8], P(('group', 'dev')), may hold values from 1 to 16
Outputs:
- new_weights: bfloat16 [128, 3584, 1024], P(('group', 'dev'))
- new_scales: bfloat16 [128, 28, 8], P(('group', 'dev'))
- hidden_out: bfloat16 [2048, 8, 1024], P(('group', 'dev'))
- slot_load: int32 [128, 3], P(('group', 'dev'))
Inputs may be any that keep to these rules, and one draw needn't show every extreme that they name: `new_place`: the redundant slots of the 16 devices of one group hold 16 different experts, each with its primary copy on a device of that group.
All inputs are finite; a program needn't handle non-finite values.
Results may differ from a plain program's by a relative error of at most 0.0057.
Values may be sent and summed in bfloat16 or wider, within the bound.
A program may use at most 192 MiB of HBM per device.

v0:
```python
import jax
import jax.numpy as jnp
from jax import lax
from jax.sharding import PartitionSpec as P

D = 3584
FF = 1024
TILE = 128
CAP = 2


def dequantize(values, scales):
    tile_grid = values.astype(jnp.float32).reshape(D // TILE, TILE, FF // TILE, TILE)
    scaled = tile_grid * scales.astype(jnp.float32)[:, None, :, None]
    return scaled.reshape(D, FF).astype(jnp.bfloat16)


def spread_parts(values, scales, parts_count):
    holding, width_in, hidden = values.shape
    split_values = values.reshape(holding, parts_count, width_in // parts_count, hidden)
    split_scales = jnp.broadcast_to(scales[:, None], (holding, parts_count) + scales.shape[1:])
    return (split_values, split_scales)


def pick_parts(got_values, got_scales, wanted, first_dev):
    holding = got_values.shape[0]
    parts_count = got_values.shape[1]
    chosen = wanted % holding * parts_count + (wanted // holding - first_dev)
    values = got_values.reshape((holding * parts_count,) + got_values.shape[2:])[chosen]
    scales = got_scales.reshape((holding * parts_count,) + got_scales.shape[2:])[chosen]
    return (values, scales)


def per_device(primary_q, primary_scales, new_place, tokens, experts, replica, route_num):
    place_all = lax.all_gather(new_place, ("group", "dev"), axis=0, tiled=True)
    holding = primary_q.shape[0]
    parts_count = lax.axis_size("dev")
    first_dev = lax.axis_index("group") * parts_count
    wanted = lax.dynamic_slice_in_dim(place_all, first_dev, parts_count)
    split_values, split_scales = spread_parts(primary_q, primary_scales, parts_count)
    got_values, got_scales = (
        lax.all_to_all(split_values, "dev", split_axis=1, concat_axis=1, tiled=True),
        lax.all_to_all(split_scales, "dev", split_axis=1, concat_axis=1, tiled=True),
    )
    send_values, send_scales = pick_parts(got_values, got_scales, wanted, first_dev)
    back_values, back_scales = (
        lax.all_to_all(send_values, "dev", split_axis=0, concat_axis=0, tiled=True),
        lax.all_to_all(send_scales, "dev", split_axis=0, concat_axis=0, tiled=True),
    )
    new_weights = back_values.reshape((1, D, FF))
    new_scales = back_scales[0:1]
    row_count, top_count = experts.shape
    pair_count = row_count * top_count
    device_count = place_all.shape[0]
    expert_flat = experts.reshape(pair_count)
    device_ids = jnp.arange(device_count, dtype=jnp.int32)
    matched = expert_flat[:, None] == place_all[None, :]
    has_copy = jnp.any(matched, axis=1)
    holder = jnp.sum(jnp.where(matched, device_ids[None, :], 0), axis=1)
    use_copy = (replica.reshape(pair_count) == 1) & has_copy
    target = jnp.where(use_copy, holder, expert_flat // holding)
    slot_id = jnp.where(use_copy, holding, expert_flat % holding)
    pair_order = jnp.arange(pair_count)
    earlier = (target[:, None] == target[None, :]) & (pair_order[None, :] < pair_order[:, None])
    position = jnp.sum(earlier, axis=1)
    served = position < CAP
    cell_count = device_count * CAP
    cell_index = target * CAP + position
    placed = (cell_index[None, :] == jnp.arange(cell_count)[:, None]) & served[None, :]
    row_hits = jnp.any(placed.reshape(cell_count, row_count, top_count), axis=2)
    row_buffer = jnp.dot(row_hits.astype(jnp.bfloat16), tokens, preferred_element_type=jnp.float32)
    row_buffer = row_buffer.astype(jnp.bfloat16).reshape(device_count, CAP, D)
    code_values = jnp.sum(jnp.where(placed, slot_id[None, :] + 1, 0), axis=1) - 1
    code_buffer = code_values.astype(jnp.float32).astype(jnp.bfloat16).reshape(device_count, CAP)
    matrices = [dequantize(primary_q[member], primary_scales[member]) for member in range(holding)]
    matrices.append(dequantize(new_weights[0], new_scales[0]))
    joined = jnp.concatenate(matrices, axis=1)
    row_block = lax.all_to_all(
        row_buffer, ("group", "dev"), split_axis=0, concat_axis=0, tiled=True
    )
    slot_codes = lax.all_to_all(
        code_buffer, ("group", "dev"), split_axis=0, concat_axis=0, tiled=True
    )
    leading, item_count, width_in = row_block.shape
    product = jnp.dot(
        row_block.reshape(leading * item_count, width_in),
        joined,
        preferred_element_type=jnp.float32,
    )
    flat_codes = slot_codes.reshape(leading * item_count).astype(jnp.float32)
    picked = jnp.zeros((leading * item_count, FF), jnp.float32)
    tallies = []
    for member in range(holding + 1):
        chosen = flat_codes == member
        picked = picked + jnp.where(
            chosen[:, None], product[:, member * FF : (member + 1) * FF], 0.0
        )
        tallies.append(chosen.astype(jnp.float32))
    activated = jax.nn.silu(picked).astype(jnp.bfloat16).reshape(leading, item_count, FF)
    activated, tallies = (
        activated,
        jnp.stack(tallies, axis=1).reshape(leading, item_count, holding + 1),
    )
    returned = lax.all_to_all(activated, ("group", "dev"), split_axis=0, concat_axis=0, tiled=True)
    dest_hit = (target[None, :] == device_ids[:, None]) & served[None, :]
    slot_hit = slot_id[:, None] == jnp.arange(holding + 1)[None, :]
    counted = jnp.dot(
        dest_hit.astype(jnp.float32), slot_hit.astype(jnp.float32), precision=lax.Precision.HIGHEST
    )
    summed = lax.psum_scatter(counted, ("group", "dev"), scatter_dimension=0, tiled=True)
    slot_load = summed.astype(jnp.int32)
    selected = jnp.dot(
        placed.T.astype(jnp.bfloat16),
        returned.reshape(cell_count, FF),
        preferred_element_type=jnp.float32,
    )
    weight = route_num.reshape(pair_count).astype(jnp.float32) / 16.0
    hidden_out = (selected * weight[:, None]).astype(jnp.bfloat16).reshape(row_count, top_count, FF)
    return (new_weights, new_scales, hidden_out, slot_load)


def solution(mesh):
    in_specs = (
        P(("group", "dev"), None, None),
        P(("group", "dev"), None, None),
        P(("group", "dev")),
        P(("group", "dev"), None),
        P(("group", "dev"), None),
        P(("group", "dev"), None),
        P(("group", "dev"), None),
    )
    out_specs = (
        P(("group", "dev"), None, None),
        P(("group", "dev"), None, None),
        P(("group", "dev"), None, None),
        P(("group", "dev"), None),
    )
    return jax.shard_map(
        per_device, mesh=mesh, in_specs=in_specs, out_specs=out_specs, check_vma=False
    )
```

profile of v0, /device:TPU:1, one launch (start us, length us, event | category | flops | bytes accessed | tf_op | source)
XLA Modules:
  0.0 594.2 jit_solution(13034104524677342891)
XLA Ops:
  0.6 0.7 broadcast_bitcast_fusion
  1.4 0.7 reshape.356
  2.1 8.4 %all-to-all-start.2 = ((bf16[16,2,224]{2,1,0:T(2,128)(2,1)}), bf16[16,2,224]{2,1,0:T(2,128)(2,1)S(1)}, u32[]{:S(2)}, u32[]{:S(2)}) async-start(bf16[16,2,224]{2,1,0:T(2,128)(2,1)} %reshape.356), calls=%async_computation.2 | async-start | bytes 32768 | tf_op jit(solution)/shard_map/all_to_all | solution.py:43
  11.3 66.6 %all-reduce = s32[128]{0:T(128)S(1)} all-reduce(s32[128]{0:T(128)S(1)} %dynamic-update-slice), channel_id=1, replica_groups=mesh['group'=8,'dev'=16] {'group','dev'}, use_global_device_ids=true, to_apply=%add | all-reduce | flops 128 | bytes 1024
  77.9 0.8 copy.62
  78.7 0.2 compare_reduce_fusion.3
  78.9 0.2 fusion.17
  79.1 0.8 copy.61
  80.0 0.2 convert_reduce_fusion
  80.2 0.1 select_reduce_fusion
  80.4 0.8 convert_element_type.161
  81.2 4.9 all-to-all-start.4
  86.3 1.2 gather_fusion.1
  87.4 8.4 %all-to-all-done.4 = bf16[128,1,2]{2,1,0:T(2,128)(2,1)S(1)} async-done(((bf16[128,1,2]{2,1,0:T(2,128)(2,1)}), bf16[128,1,2]{2,1,0:T(2,128)(2,1)S(1)}, u32[]{:S(2)}, u32[]{:S(2)}) %all-to-all-start.4) | async-done | bytes 544 | tf_op jit(solution)/shard_map/all_to_all | solution.py:81
  95.8 3.5 all-to-all-start.3
  99.3 13.7 %copy.58 = bf16[2,16,224,1024]{3,2,0,1:T(8,128)(2,1)} copy(bf16[2,16,224,1024]{3,2,1,0:T(8,128)(2,1)} %bitcast.49) | data formatting | bytes 29360128 | tf_op jit(solution)/shard_map/reshape | solution.py:20
  113.0 6.6 %all-to-all-start = ((bf16[2,16,224,1024]{3,2,0,1:T(8,128)(2,1)}), bf16[2,16,224,1024]{3,2,0,1:T(8,128)(2,1)}, u32[]{:S(2)}, u32[]{:S(2)}) async-start(bf16[2,16,224,1024]{3,2,0,1:T(8,128)(2,1)} %copy.58), calls=%async_computation | async-start | bytes 29360128 | tf_op jit(solution)/shard_map/all_to_all | solution.py:42
  120.0 0.1 fusion.16
  120.1 0.7 convolution_convert_fusion
  120.8 1.7 reshape.322
  122.5 212.4 %all-to-all-done = bf16[2,16,224,1024]{3,2,0,1:T(8,128)(2,1)} async-done(((bf16[2,16,224,1024]{3,2,0,1:T(8,128)(2,1)}), bf16[2,16,224,1024]{3,2,0,1:T(8,128)(2,1)}, u32[]{:S(2)}, u32[]{:S(2)}) %all-to-all-start) | async-done | bytes 14680096 | tf_op jit(solution)/shard_map/all_to_all | solution.py:42
  334.9 7.7 %all-to-all-start.5 = ((bf16[128,2,3584]{2,1,0:T(2,128)(2,1)}), bf16[128,2,3584]{2,1,0:T(2,128)(2,1)S(1)}, u32[]{:S(2)}, u32[]{:S(2)}) async-start(bf16[128,2,3584]{2,1,0:T(2,128)(2,1)} %reshape.322), calls=%async_computation.5 | async-start | bytes 3670016 | tf_op jit(solution)/shard_map/all_to_all | solution.py:78
  342.5 13.7 %copy.59 = bf16[2,16,224,1024]{3,2,1,0:T(8,128)(2,1)} copy(bf16[2,16,224,1024]{3,2,0,1:T(8,128)(2,1)} %all-to-all-done) | data formatting | bytes 29360128 | tf_op jit(solution)/shard_map/all_to_all | solution.py:42
  356.2 9.2 %gather_fusion = bf16[16,224,1024]{2,1,0:T(8,128)(2,1)} fusion(bf16[32,224,1024]{2,1,0:T(8,128)(2,1)} %bitcast.53, s32[1024]{0:T(1024)S(1)} %pad_clamp_fusion), kind=kCustom, calls=%fused_computation | custom fusion | bytes 14680128 | tf_op jit(solution)/shard_map/gather | solution.py:29
  365.5 3.9 all-to-all-done.5
  369.4 4.9 all-to-all-start.1
  374.5 1.0 mul.65
  375.5 6.2 %mul.68 = f32[28,128,8,128]{3,2,1,0:T(8,128)} broadcast(f32[28,8]{1,0:T(8,128)S(1)} %copy.69), dimensions={0,2} | broadcast | bytes 14680960 | tf_op jit(solution)/shard_map/mul | solution.py:14
  381.7 18.6 %fusion.8 = (bf16[3584,1024]{1,0:T(8,128)(2,1)}, bf16[3584,1024]{1,0:T(8,128)(2,1)}) fusion(f32[448,8,8,128]{3,2,1,0:T(8,128)S(1)} %bitcast.50, bf16[2,3584,1024]{2,1,0:T(8,128)(2,1)} %param.7, f32[448,8,8,128]{3,2,1,0:T(8,128)} %bitcast.51), kind=kLoop, calls=%fused_computation.13 | loop fusion | flops 22020096 | bytes 58720256 | tf_op jit(solution)/shard_map/convert_element_type | solution.py:15
  400.3 0.6 compare_reduce_fusion.2
  401.0 0.1 eq.167
  401.1 0.1 eq.164
  401.3 0.1 eq.158
  401.4 0.6 bitcast_convert_fusion
  402.1 1.7 reshape.323
  403.8 77.2 %all-to-all-done.1 = bf16[16,224,1024]{2,1,0:T(8,128)(2,1)} async-done(((bf16[16,224,1024]{2,1,0:T(8,128)(2,1)}), bf16[16,224,1024]{2,1,0:T(8,128)(2,1)}, u32[]{:S(2)}, u32[]{:S(2)}) %all-to-all-start.1) | async-done | bytes 7340064 | tf_op jit(solution)/shard_map/all_to_all | solution.py:47
  480.9 1.0 mul.71
  482.0 9.2 %fusion.6 = bf16[3584,1024]{1,0:T(8,128)(2,1)} fusion(f32[448,8,8,128]{3,2,1,0:T(8,128)S(1)} %bitcast.52, bf16[16,224,1024]{2,1,0:T(8,128)(2,1)} %all-to-all-done.1), kind=kLoop, calls=%fused_computation.9 | loop fusion | flops 11010048 | bytes 29360128 | tf_op jit(solution)/shard_map/convert_element_type | solution.py:15
  491.2 15.5 %fusion = f32[256,3072]{1,0:T(8,128)S(1)} fusion(bf16[256,3584]{1,0:T(8,128)(2,1)S(1)} %copy-done.2, bf16[3584,1024]{1,0:T(8,128)(2,1)} %fusion.6, bf16[3584,1024]{1,0:T(8,128)(2,1)} %get-tuple-element.12, bf16[3584,1024]{1,0:T(8,128)(2,1)S(1)} %bitcast.55), kind=kOutput, calls=%fused_computation.2 | convolution fusion | flops 5703204864 | bytes 27000832 | tf_op jit(solution)/shard_map/dot_general | solution.py:85
  506.8 0.5 multiply_convert_fusion
  507.2 1.0 reshape.324
  508.2 9.2 %all-to-all-start.6 = ((bf16[128,2,1024]{2,1,0:T(2,128)(2,1)}), bf16[128,2,1024]{2,1,0:T(2,128)(2,1)S(1)}, u32[]{:S(2)}, u32[]{:S(2)}) async-start(bf16[128,2,1024]{2,1,0:T(2,128)(2,1)} %reshape.324), calls=%async_computation.6 | async-start | bytes 1048576 | tf_op jit(solution)/shard_map/all_to_all | solution.py:104
  517.6 0.2 fusion.21
  517.8 67.6 %all-reduce.1 = f32[128,3]{1,0:T(8,128)S(1)} all-reduce(f32[128,3]{1,0:T(8,128)S(1)} %fusion.21), channel_id=2, replica_groups=mesh['group'=8,'dev'=16] {'group','dev'}, use_global_device_ids=true, to_apply=%region_5.6.clone | all-reduce | flops 384 | bytes 3072
  585.4 0.5 dynamic-slice_convert_fusion
  586.0 0.2 reshape.325
  586.2 1.0 fusion.10
  587.1 7.0 %copy.81 = bf16[1,3584,1024]{2,1,0:T(8,128)(2,1)} copy(bf16[1,3584,1024]{2,1,0:T(8,128)(2,1)} %bitcast.2) | data formatting | bytes 14680064
  (43 shorter events, 1.3 us)
Async XLA Ops:
  0.6 119.5 %copy-start = (bf16[16,3584]{1,0:T(8,128)(2,1)S(1)}, bf16[16,3584]{1,0:T(8,128)(2,1)}, u32[]{:S(2)}) copy-start(bf16[16,3584]{1,0:T(8,128)(2,1)} %param.10) | copy-start | bytes 344068
  2.1 79.1 %all-to-all-start.2 = ((bf16[16,2,224]{2,1,0:T(2,128)(2,1)}), bf16[16,2,224]{2,1,0:T(2,128)(2,1)S(1)}, u32[]{:S(2)}, u32[]{:S(2)}) async-start(bf16[16,2,224]{2,1,0:T(2,128)(2,1)} %reshape.356), calls=%async_computation.2 | async-start | bytes 32768 | tf_op jit(solution)/shard_map/all_to_all | solution.py:43
  81.2 14.6 %all-to-all-start.4 = ((bf16[128,1,2]{2,1,0:T(2,128)(2,1)}), bf16[128,1,2]{2,1,0:T(2,128)(2,1)S(1)}, u32[]{:S(2)}, u32[]{:S(2)}) async-start(bf16[128,1,2]{2,1,0:T(2,128)(2,1)} %convert_element_type.161), calls=%async_computation.4 | async-start | bytes 131072 | tf_op jit(solution)/shard_map/all_to_all | solution.py:81
  95.8 17.2 %all-to-all-start.3 = ((bf16[16,28,8]{1,2,0:T(8,128)(2,1)}), bf16[16,28,8]{1,2,0:T(8,128)(2,1)S(1)}, u32[]{:S(2)}, u32[]{:S(2)}) async-start(bf16[16,28,8]{1,2,0:T(8,128)(2,1)} %gather_fusion.1), calls=%async_computation.3 | async-start | bytes 65536 | tf_op jit(solution)/shard_map/all_to_all | solution.py:48
  113.0 221.8 %all-to-all-start = ((bf16[2,16,224,1024]{3,2,0,1:T(8,128)(2,1)}), bf16[2,16,224,1024]{3,2,0,1:T(8,128)(2,1)}, u32[]{:S(2)}, u32[]{:S(2)}) async-start(bf16[2,16,224,1024]{3,2,0,1:T(8,128)(2,1)} %copy.58), calls=%async_computation | async-start | bytes 29360128 | tf_op jit(solution)/shard_map/all_to_all | solution.py:42
  334.9 34.5 %all-to-all-start.5 = ((bf16[128,2,3584]{2,1,0:T(2,128)(2,1)}), bf16[128,2,3584]{2,1,0:T(2,128)(2,1)S(1)}, u32[]{:S(2)}, u32[]{:S(2)}) async-start(bf16[128,2,3584]{2,1,0:T(2,128)(2,1)} %reshape.322), calls=%async_computation.5 | async-start | bytes 3670016 | tf_op jit(solution)/shard_map/all_to_all | solution.py:78
  365.5 8.8 %copy-start.3 = (bf16[2,28,8]{1,2,0:T(8,128)(2,1)S(1)}, bf16[2,28,8]{1,2,0:T(8,128)(2,1)}, u32[]{:S(2)}) copy-start(bf16[2,28,8]{1,2,0:T(8,128)(2,1)} %param.8) | copy-start | bytes 2692
  369.4 111.5 %all-to-all-start.1 = ((bf16[16,224,1024]{2,1,0:T(8,128)(2,1)}), bf16[16,224,1024]{2,1,0:T(8,128)(2,1)}, u32[]{:S(2)}, u32[]{:S(2)}) async-start(bf16[16,224,1024]{2,1,0:T(8,128)(2,1)} %gather_fusion), calls=%async_computation.1 | async-start | bytes 14680064 | tf_op jit(solution)/shard_map/all_to_all | solution.py:47
  480.9 10.3 %slice-start = ((s8[7340032]{0:T(1024)(128)(4,1)}), s8[4194304]{0:T(1024)(128)(4,1)S(1)}, s32[]{:S(2)}) async-start(s8[7340032]{0:T(1024)(128)(4,1)} %bitcast.54), calls=%async_computation.7 | async-start | bytes 8388608
  481.9 9.3 %slice-start.1 = ((s8[7340032]{0:T(1024)(128)(4,1)}), s8[3145728]{0:T(1024)(128)(4,1)S(1)}, s32[]{:S(2)}) async-start(s8[7340032]{0:T(1024)(128)(4,1)} %bitcast.54), calls=%async_computation.8 | async-start | bytes 6291456
  481.9 9.3 %copy-start.2 = (bf16[256,3584]{1,0:T(8,128)(2,1)S(1)}, bf16[256,3584]{1,0:T(8,128)(2,1)}, u32[]{:S(2)}) copy-start(bf16[256,3584]{1,0:T(8,128)(2,1)} %reshape.323) | copy-start | bytes 5505028
  491.2 26.2 %copy-start.4 = (s32[16,8]{0,1:T(8,128)S(1)}, s32[16,8]{0,1:T(8,128)}, u32[]{:S(2)}) copy-start(s32[16,8]{0,1:T(8,128)} %param.13) | copy-start | bytes 1540
  508.2 77.7 %all-to-all-start.6 = ((bf16[128,2,1024]{2,1,0:T(2,128)(2,1)}), bf16[128,2,1024]{2,1,0:T(2,128)(2,1)S(1)}, u32[]{:S(2)}, u32[]{:S(2)}) async-start(bf16[128,2,1024]{2,1,0:T(2,128)(2,1)} %reshape.324), calls=%async_computation.6 | async-start | bytes 1048576 | tf_op jit(solution)/shard_map/all_to_all | solution.py:104
  587.1 7.0 %copy-start.1 = (bf16[16,3584]{1,0:T(8,128)(2,1)S(1)}, bf16[16,3584]{1,0:T(8,128)(2,1)}, u32[]{:S(2)}) copy-start(bf16[16,3584]{1,0:T(8,128)(2,1)} %param.10) | copy-start | bytes 344068
where the time goes:
time: 595 us; the launch traced here: 594 us
  waiting for transfers between devices  302 us (51%)
  blocking collectives  134 us (23%)
  local copies, waits for them, and re-layouts  63 us (11%)
  starting transfers between devices  45.2 us (8%)
  other arithmetic  31 us (5%)
  matrix products  17.4 us (3%)
    all_to_all x1, waiting for transfers between devices, per_device(): lax.all_to_all(split_values, 'dev', split_axis=1, concat_axis=1, tiled=True)  212 us
    unnamed x2, blocking collectives  134 us
    all_to_all x1, waiting for transfers between devices, per_device(): lax.all_to_all(send_values, 'dev', split_axis=0, concat_axis=0, tiled=True)  77.2 us
    convert_element_type x2, other arithmetic, dequantize(): return scaled.reshape(D, FF).astype(jnp.bfloat16)  27.9 us
    dot_general x1, matrix products, per_device(): jnp.dot(row_block.reshape(leading * item_count, width_in), joined, prefer...  15.5 us
    reshape x1, local copies, waits for them, and re-layouts, spread_parts(): values.reshape(holding, parts_count, width_in // parts_count, hidden)  13.7 us
    all_to_all x1, local copies, waits for them, and re-layouts, per_device(): lax.all_to_all(split_values, 'dev', split_axis=1, concat_axis=1, tiled=True)  13.7 us
  transfers between devices with their start and end apart: 7, of which 4 were waited for; matrix products, arithmetic and copies ran while one was open for 13% of the time, Pallas kernels for 0%

commit v1 on v0

--- a/solution.py
+++ b/solution.py
@@ -39,7 +39,12 @@
     wanted = lax.dynamic_slice_in_dim(place_all, first_dev, parts_count)
     split_values, split_scales = spread_parts(primary_q, primary_scales, parts_count)
     got_values, got_scales = (
-        lax.all_to_all(split_values, "dev", split_axis=1, concat_axis=1, tiled=True),
+        jnp.concatenate(
+            lax.all_to_all(
+                jnp.stack(jnp.split(split_values, lax.axis_size("dev"), axis=1)), "dev", 0, 0
+            ),
+            axis=1,
+        ),
         lax.all_to_all(split_scales, "dev", split_axis=1, concat_axis=1, tiled=True),
     )
     send_values, send_scales = pick_parts(got_values, got_scales, wanted, first_dev)

time: 595 us -> 618 us (1.039)
  local copies, waits for them, and re-layouts: 63 us -> 84.2 us
    unnamed x22 -> x37, local copies, waits for them, and re-layouts: 10.3 us -> 43 us
    all_to_all x1 -> x0, local copies, waits for them, and re-layouts: 13.7 us -> none  [per_device(): lax.all_to_all(split_values, 'dev', split_axis=1, concat_axis=1, tiled=True)]
  transfers between devices with their start and end apart: 7 -> 7, of which waited for: 4 -> 5; matrix products, arithmetic and copies ran while one was open for 13% -> 16% of each run, Pallas kernels for 0% -> 0%
where the time goes in v1:
time: 618 us; the launch traced here: 617 us
  waiting for transfers between devices  303 us (49%)
  blocking collectives  134 us (22%)
  local copies, waits for them, and re-layouts  84.2 us (14%)
  starting transfers between devices  45.1 us (7%)
  other arithmetic  31 us (5%)
  matrix products  17.4 us (3%)
    all_to_all x1, waiting for transfers between devices, per_device(): lax.all_to_all(jnp.stack(jnp.split(split_values, lax.axis_size('dev'), ax...  210 us
    unnamed x2, blocking collectives  134 us
    all_to_all x1, waiting for transfers between devices, per_device(): lax.all_to_all(send_values, 'dev', split_axis=0, concat_axis=0, tiled=True)  77.2 us
    unnamed x37, local copies, waits for them, and re-layouts  43 us
    convert_element_type x2, other arithmetic, dequantize(): return scaled.reshape(D, FF).astype(jnp.bfloat16)  27.9 us
    dot_general x1, matrix products, per_device(): jnp.dot(row_block.reshape(leading * item_count, width_in), joined, prefer...  15.5 us
    reshape x1, local copies, waits for them, and re-layouts, per_device(): jnp.concatenate(lax.all_to_all(jnp.stack(jnp.split(split_values, lax.axis...  13.7 us
  transfers between devices with their start and end apart: 7, of which 5 were waited for; matrix products, arithmetic and copies ran while one was open for 16% of the time, Pallas kernels for 0%

profile of v1, /device:TPU:1, one launch (start us, length us, event | category | flops | bytes accessed | tf_op | source)
XLA Modules:
  0.0 616.9 jit_solution(696003792702877784)
XLA Ops:
  1.4 0.7 reshape.356
  2.1 8.4 %all-to-all-start.2 = ((bf16[16,2,224]{2,1,0:T(2,128)(2,1)}), bf16[16,2,224]{2,1,0:T(2,128)(2,1)S(1)}, u32[]{:S(2)}, u32[]{:S(2)}) async-start(bf16[16,2,224]{2,1,0:T(2,128)(2,1)} %reshape.356), calls=%async_computation.2 | async-start | bytes 32768 | tf_op jit(solution)/shard_map/all_to_all | solution.py:48
  11.3 66.6 %all-reduce = s32[128]{0:T(128)S(1)} all-reduce(s32[128]{0:T(128)S(1)} %dynamic-update-slice), channel_id=1, replica_groups=mesh['group'=8,'dev'=16] {'group','dev'}, use_global_device_ids=true, to_apply=%add | all-reduce | flops 128 | bytes 1024
  77.9 0.8 copy.134
  79.1 0.8 copy.133
  80.2 2.2 fusion.28
  82.4 2.2 fusion.27
  84.6 2.2 fusion.26
  86.7 2.2 fusion.25
  88.9 2.2 fusion.24
  91.1 2.2 fusion.23
  93.2 2.2 fusion.22
  95.4 2.2 fusion.21
  97.6 2.2 fusion.20
  99.8 2.2 fusion.19
  101.9 2.2 fusion.18
  104.1 2.3 fusion.17
  106.4 2.2 fusion.16
  108.6 2.2 fusion.15
  110.8 2.2 fusion.14
  113.2 0.8 convert_element_type.161
  114.0 4.9 all-to-all-start.4
  119.0 1.2 gather_fusion.1
  120.2 8.4 %all-to-all-done.4 = bf16[128,1,2]{2,1,0:T(2,128)(2,1)S(1)} async-done(((bf16[128,1,2]{2,1,0:T(2,128)(2,1)}), bf16[128,1,2]{2,1,0:T(2,128)(2,1)S(1)}, u32[]{:S(2)}, u32[]{:S(2)}) %all-to-all-start.4) | async-done | bytes 544 | tf_op jit(solution)/shard_map/all_to_all | solution.py:86
  128.6 3.5 all-to-all-start.3
  132.1 2.2 fusion.13
  134.3 4.2 all-to-all-done.3
  138.5 5.0 all-to-all-start
  144.6 1.7 reshape.322
  146.3 209.8 %all-to-all-done = bf16[16,2,1,224,1024]{4,3,1,2,0:T(8,128)(2,1)} async-done(((bf16[16,2,1,224,1024]{4,3,1,2,0:T(8,128)(2,1)}), bf16[16,2,1,224,1024]{4,3,1,2,0:T(8,128)(2,1)}, u32[]{:S(2)}, u32[]{:S(2)}) %all-to-all-start) | async-done | bytes 14680096 | tf_op jit(solution)/shard_map/all_to_all | solution.py:43
  356.1 9.3 %all-to-all-start.5 = ((bf16[128,2,3584]{2,1,0:T(2,128)(2,1)}), bf16[128,2,3584]{2,1,0:T(2,128)(2,1)S(1)}, u32[]{:S(2)}, u32[]{:S(2)}) async-start(bf16[128,2,3584]{2,1,0:T(2,128)(2,1)} %reshape.322), calls=%async_computation.5 | async-start | bytes 3670016 | tf_op jit(solution)/shard_map/all_to_all | solution.py:83
  365.4 13.7 %copy.131 = bf16[2,16,1,224,1024]{4,3,1,0,2:T(8,128)(2,1)} copy(bf16[2,16,1,224,1024]{4,3,0,2,1:T(8,128)(2,1)} %bitcast.17) | data formatting | bytes 29360128 | tf_op jit(solution)/shard_map/reshape | solution.py:42
  379.1 9.2 %gather_fusion = bf16[16,224,1024]{2,1,0:T(8,128)(2,1)} fusion(bf16[32,224,1024]{2,1,0:T(8,128)(2,1)} %bitcast.163, s32[1024]{0:T(1024)S(1)} %pad_clamp_fusion), kind=kCustom, calls=%fused_computation | custom fusion | bytes 14680128 | tf_op jit(solution)/shard_map/gather | solution.py:29
  388.4 3.9 all-to-all-done.5
  392.3 4.9 all-to-all-start.1
  397.4 1.0 mul.65
  398.4 6.2 %mul.68 = f32[28,128,8,128]{3,2,1,0:T(8,128)} broadcast(f32[28,8]{1,0:T(8,128)S(1)} %copy.141), dimensions={0,2} | broadcast | bytes 14680960 | tf_op jit(solution)/shard_map/mul | solution.py:14
  404.6 18.6 %fusion.8 = (bf16[3584,1024]{1,0:T(8,128)(2,1)}, bf16[3584,1024]{1,0:T(8,128)(2,1)}) fusion(f32[448,8,8,128]{3,2,1,0:T(8,128)S(1)} %bitcast.144, bf16[2,3584,1024]{2,1,0:T(8,128)(2,1)} %param.7, f32[448,8,8,128]{3,2,1,0:T(8,128)} %bitcast.145), kind=kLoop, calls=%fused_computation.13 | loop fusion | flops 22020096 | bytes 58720256 | tf_op jit(solution)/shard_map/convert_element_type | solution.py:15
  425.0 1.7 reshape.323
  426.7 77.2 %all-to-all-done.1 = bf16[16,224,1024]{2,1,0:T(8,128)(2,1)} async-done(((bf16[16,224,1024]{2,1,0:T(8,128)(2,1)}), bf16[16,224,1024]{2,1,0:T(8,128)(2,1)}, u32[]{:S(2)}, u32[]{:S(2)}) %all-to-all-start.1) | async-done | bytes 7340064 | tf_op jit(solution)/shard_map/all_to_all | solution.py:52
  503.8 1.0 mul.71
  504.9 9.2 %fusion.6 = bf16[3584,1024]{1,0:T(8,128)(2,1)} fusion(f32[448,8,8,128]{3,2,1,0:T(8,128)S(1)} %bitcast.146, bf16[16,224,1024]{2,1,0:T(8,128)(2,1)} %all-to-all-done.1), kind=kLoop, calls=%fused_computation.9 | loop fusion | flops 11010048 | bytes 29360128 | tf_op jit(solution)/shard_map/convert_element_type | solution.py:15
  514.1 15.5 %fusion = f32[256,3072]{1,0:T(8,128)S(1)} fusion(bf16[256,3584]{1,0:T(8,128)(2,1)S(1)} %copy-done.2, bf16[3584,1024]{1,0:T(8,128)(2,1)} %fusion.6, bf16[3584,1024]{1,0:T(8,128)(2,1)} %get-tuple-element.12, bf16[3584,1024]{1,0:T(8,128)(2,1)S(1)} %bitcast.165), kind=kOutput, calls=%fused_computation.2 | convolution fusion | flops 5703204864 | bytes 27000832 | tf_op jit(solution)/shard_map/dot_general | solution.py:90
  530.1 1.0 reshape.324
  531.1 9.0 %all-to-all-start.6 = ((bf16[128,2,1024]{2,1,0:T(2,128)(2,1)}), bf16[128,2,1024]{2,1,0:T(2,128)(2,1)S(1)}, u32[]{:S(2)}, u32[]{:S(2)}) async-start(bf16[128,2,1024]{2,1,0:T(2,128)(2,1)} %reshape.324), calls=%async_computation.6 | async-start | bytes 1048576 | tf_op jit(solution)/shard_map/all_to_all | solution.py:109
  540.6 67.6 %all-reduce.1 = f32[128,3]{1,0:T(8,128)S(1)} all-reduce(f32[128,3]{1,0:T(8,128)S(1)} %fusion.37), channel_id=2, replica_groups=mesh['group'=8,'dev'=16] {'group','dev'}, use_global_device_ids=true, to_apply=%region_5.6.clone | all-reduce | flops 384 | bytes 3072
  608.9 1.0 fusion.10
  609.9 7.0 %copy.183 = bf16[1,3584,1024]{2,1,0:T(8,128)(2,1)} copy(bf16[1,3584,1024]{2,1,0:T(8,128)(2,1)} %bitcast.19) | data formatting | bytes 14680064
  (58 shorter events, 6.5 us)
Async XLA Ops:
  0.6 143.3 %copy-start = (bf16[16,3584]{1,0:T(8,128)(2,1)S(1)}, bf16[16,3584]{1,0:T(8,128)(2,1)}, u32[]{:S(2)}) copy-start(bf16[16,3584]{1,0:T(8,128)(2,1)} %param.10) | copy-start | bytes 344068
  2.1 111.9 %all-to-all-start.2 = ((bf16[16,2,224]{2,1,0:T(2,128)(2,1)}), bf16[16,2,224]{2,1,0:T(2,128)(2,1)S(1)}, u32[]{:S(2)}, u32[]{:S(2)}) async-start(bf16[16,2,224]{2,1,0:T(2,128)(2,1)} %reshape.356), calls=%async_computation.2 | async-start | bytes 32768 | tf_op jit(solution)/shard_map/all_to_all | solution.py:48
  114.0 14.6 %all-to-all-start.4 = ((bf16[128,1,2]{2,1,0:T(2,128)(2,1)}), bf16[128,1,2]{2,1,0:T(2,128)(2,1)S(1)}, u32[]{:S(2)}, u32[]{:S(2)}) async-start(bf16[128,1,2]{2,1,0:T(2,128)(2,1)} %convert_element_type.161), calls=%async_computation.4 | async-start | bytes 131072 | tf_op jit(solution)/shard_map/all_to_all | solution.py:86
  128.6 9.9 %all-to-all-start.3 = ((bf16[16,28,8]{1,2,0:T(8,128)(2,1)}), bf16[16,28,8]{1,2,0:T(8,128)(2,1)S(1)}, u32[]{:S(2)}, u32[]{:S(2)}) async-start(bf16[16,28,8]{1,2,0:T(8,128)(2,1)} %gather_fusion.1), calls=%async_computation.3 | async-start | bytes 65536 | tf_op jit(solution)/shard_map/all_to_all | solution.py:53
  138.5 217.6 %all-to-all-start = ((bf16[16,2,1,224,1024]{4,3,1,2,0:T(8,128)(2,1)}), bf16[16,2,1,224,1024]{4,3,1,2,0:T(8,128)(2,1)}, u32[]{:S(2)}, u32[]{:S(2)}) async-start(bf16[16,2,1,224,1024]{4,3,1,2,0:T(8,128)(2,1)} %fusion.13), calls=%async_computation | async-start | bytes 29360128 | tf_op jit(solution)/shard_map/all_to_all | solution.py:43
  356.1 36.2 %all-to-all-start.5 = ((bf16[128,2,3584]{2,1,0:T(2,128)(2,1)}), bf16[128,2,3584]{2,1,0:T(2,128)(2,1)S(1)}, u32[]{:S(2)}, u32[]{:S(2)}) async-start(bf16[128,2,3584]{2,1,0:T(2,128)(2,1)} %reshape.322), calls=%async_computation.5 | async-start | bytes 3670016 | tf_op jit(solution)/shard_map/all_to_all | solution.py:83
  379.1 18.0 %copy-start.3 = (bf16[2,28,8]{1,2,0:T(8,128)(2,1)S(1)}, bf16[2,28,8]{1,2,0:T(8,128)(2,1)}, u32[]{:S(2)}) copy-start(bf16[2,28,8]{1,2,0:T(8,128)(2,1)} %param.8) | copy-start | bytes 2692
  392.3 111.5 %all-to-all-start.1 = ((bf16[16,224,1024]{2,1,0:T(8,128)(2,1)}), bf16[16,224,1024]{2,1,0:T(8,128)(2,1)}, u32[]{:S(2)}, u32[]{:S(2)}) async-start(bf16[16,224,1024]{2,1,0:T(8,128)(2,1)} %gather_fusion), calls=%async_computation.1 | async-start | bytes 14680064 | tf_op jit(solution)/shard_map/all_to_all | solution.py:52
  503.8 10.3 %slice-start = ((s8[7340032]{0:T(1024)(128)(4,1)}), s8[4194304]{0:T(1024)(128)(4,1)S(1)}, s32[]{:S(2)}) async-start(s8[7340032]{0:T(1024)(128)(4,1)} %bitcast.164), calls=%async_computation.7 | async-start | bytes 8388608
  504.8 9.3 %slice-start.1 = ((s8[7340032]{0:T(1024)(128)(4,1)}), s8[3145728]{0:T(1024)(128)(4,1)S(1)}, s32[]{:S(2)}) async-start(s8[7340032]{0:T(1024)(128)(4,1)} %bitcast.164), calls=%async_computation.8 | async-start | bytes 6291456
  504.9 9.3 %copy-start.2 = (bf16[256,3584]{1,0:T(8,128)(2,1)S(1)}, bf16[256,3584]{1,0:T(8,128)(2,1)}, u32[]{:S(2)}) copy-start(bf16[256,3584]{1,0:T(8,128)(2,1)} %reshape.323) | copy-start | bytes 5505028
  514.1 26.1 %copy-start.4 = (s32[16,8]{0,1:T(8,128)S(1)}, s32[16,8]{0,1:T(8,128)}, u32[]{:S(2)}) copy-start(s32[16,8]{0,1:T(8,128)} %param.13) | copy-start | bytes 1540
  514.1 102.7 %copy-start.1 = (bf16[16,3584]{1,0:T(8,128)(2,1)S(1)}, bf16[16,3584]{1,0:T(8,128)(2,1)}, u32[]{:S(2)}) copy-start(bf16[16,3584]{1,0:T(8,128)(2,1)} %param.10) | copy-start | bytes 344068
  531.1 77.6 %all-to-all-start.6 = ((bf16[128,2,1024]{2,1,0:T(2,128)(2,1)}), bf16[128,2,1024]{2,1,0:T(2,128)(2,1)S(1)}, u32[]{:S(2)}, u32[]{:S(2)}) async-start(bf16[128,2,1024]{2,1,0:T(2,128)(2,1)} %reshape.324), calls=%async_computation.6 | async-start | bytes 1048576 | tf_op jit(solution)/shard_map/all_to_all | solution.py:109
